TPU v7x, 32 devices: a whole 2x2x4 slice. The times are simulated.
32 devices in a mesh: ctx: 2 (over x), fsdp: 16 (over z, y, core).
Axes of the slice: x: 2, y: 2, z: 4, core: 2. Of those that a mesh axis runs over, the one named last changes fastest.
Arguments:
- hidden_in: bfloat16 [16, 256, 1280], P('fsdp', 'ctx'), may hold values from -8 to 8
- values: bfloat16 [16, 256, 2560], P('fsdp', 'ctx'), may hold values from -6 to 6
- log_decay: float32 [16, 40, 256], P('fsdp', None, 'ctx'), may hold values from -1 to 0, as said below
- doc_lengths: int32 [16, 4], P('fsdp'), may hold values from 1 to 128, 256 in all within a row
- proj_bc: bfloat16 [1280, 256], P('fsdp'), may hold values from -0.15625 to 0.15625
- grad_out: bfloat16 [16, 256, 2560], P('fsdp', 'ctx'), may hold values from -6 to 6
Outputs:
- grad_values: bfloat16 [16, 256, 2560], P('fsdp', 'ctx')
- grad_hidden: bfloat16 [16, 256, 1280], P('fsdp', 'ctx')
- grad_proj: float32 [1280, 256], P('fsdp')
Inputs may be any that keep to these rules, and one draw needn't show every extreme that they name: `doc_lengths`: each sequence's 4 document lengths sum to 256; the longest is exactly half of 256. `log_decay`: logarithms of decays, all negative.
All inputs are finite; a program needn't handle non-finite values.
Results may differ from a plain program's by a relative error of at most 0.012.
Values may be sent and summed in bfloat16 or wider, within the bound.
A program may use at most 64 MiB of HBM per device.

v0:
```python
import jax
import jax.numpy as jnp
from jax import lax
from jax.sharding import PartitionSpec as P


def entering(value, axis, combine, identity, reverse):
    length, mine = (lax.axis_size(axis), lax.axis_index(axis))
    everything = jax.tree.map(
        lambda part, kind: lax.all_gather(part.astype(kind), axis),
        value,
        (jnp.bfloat16, jnp.bfloat16),
    )
    start = jax.tree.map(
        lambda part, zero: jnp.broadcast_to(jnp.asarray(zero, part.dtype), part.shape),
        value,
        identity,
    )

    def turn(k, before):
        at = length - 1 - k if reverse else k
        reached = at > mine if reverse else at < mine
        new = combine(
            before, jax.tree.map(lambda part, own: part[at].astype(own.dtype), everything, value)
        )
        return jax.tree.map(lambda a, b: jnp.where(reached, a, b), new, before)

    return lax.fori_loop(0, length, turn, start)


def combine_pairs(first_pair, second_pair):
    first_decay, first_state = first_pair
    second_decay, second_state = second_pair
    rows_count = first_state.shape[0]
    head_count = first_decay.shape[0]
    decayed = (
        first_state.reshape(rows_count, head_count, -1) * second_decay[None, :, None]
    ).reshape(first_state.shape)
    return (first_decay * second_decay, decayed + second_state)


def block_terms(b_rows, c_rows, value_rows, grad_rows, decay_rows, doc_ids, prev_doc):
    token_count, state_size = b_rows.shape
    head_count = decay_rows.shape[0]
    inner_width = value_rows.shape[1]
    head_dim = inner_width // head_count
    cumulative = jnp.cumsum(decay_rows, axis=1)
    last_doc = doc_ids[-1]
    token_places = jnp.arange(token_count, dtype=jnp.int32)
    allowed = (doc_ids[:, None] == doc_ids[None, :]) & (
        token_places[:, None] >= token_places[None, :]
    )
    spread = cumulative[:, :, None] - cumulative[:, None, :]
    decay_matrix = jnp.where(allowed[None], jnp.exp(jnp.where(allowed[None], spread, 0.0)), 0.0)
    in_weight = jnp.exp(cumulative) * (doc_ids == prev_doc).astype(jnp.float32)[None, :]
    out_weight = (
        jnp.exp(cumulative[:, -1:] - cumulative)
        * (doc_ids == last_doc).astype(jnp.float32)[None, :]
    )
    total_decay = jnp.exp(cumulative[:, -1]) * (last_doc == prev_doc).astype(jnp.float32)
    contract_last = (((1,), (1,)), ((), ()))
    scores = (
        lax.dot_general(c_rows, b_rows, contract_last, preferred_element_type=jnp.float32)
        / state_size
    )
    mixing = (decay_matrix * scores[None]).astype(jnp.bfloat16)
    value_heads = value_rows.reshape(token_count, head_count, head_dim)
    grad_heads = grad_rows.reshape(token_count, head_count, head_dim)
    products = jnp.einsum(
        "rhp,thp->hrt", grad_heads, value_heads, preferred_element_type=jnp.float32
    )
    kernel = (jnp.sum(decay_matrix * products, axis=0) / state_size).astype(jnp.bfloat16)
    grad_value_local = jnp.einsum(
        "hrt,rhp->thp", mixing, grad_heads, preferred_element_type=jnp.float32
    ).reshape(token_count, inner_width)
    contract_first = (((0,), (0,)), ((), ()))
    grad_b_local = lax.dot_general(
        kernel, c_rows, contract_first, preferred_element_type=jnp.float32
    )
    grad_c_local = jnp.dot(kernel, b_rows, preferred_element_type=jnp.float32)
    weighted_values = (
        (out_weight.T[:, :, None] * value_heads)
        .reshape(token_count, inner_width)
        .astype(jnp.bfloat16)
    )
    weighted_grads = (
        (in_weight.T[:, :, None] * grad_heads)
        .reshape(token_count, inner_width)
        .astype(jnp.bfloat16)
    )
    local_state = lax.dot_general(
        b_rows, weighted_values, contract_first, preferred_element_type=jnp.float32
    )
    local_grad = (
        lax.dot_general(c_rows, weighted_grads, contract_first, preferred_element_type=jnp.float32)
        / state_size
    )
    return (
        total_decay,
        local_state,
        local_grad,
        out_weight,
        weighted_values,
        weighted_grads,
        grad_value_local,
        grad_b_local,
        grad_c_local,
    )


def block_finish(b_rows, terms, state_in, grad_after):
    out_weight = terms[3]
    weighted_values = terms[4]
    weighted_grads = terms[5]
    grad_value_local = terms[6]
    grad_b_local = terms[7]
    grad_c_local = terms[8]
    token_count, state_size = b_rows.shape
    head_count = out_weight.shape[0]
    inner_width = weighted_values.shape[1]
    state_used = state_in.astype(jnp.bfloat16)
    grad_used = grad_after.astype(jnp.bfloat16)
    contract_last = (((1,), (1,)), ((), ()))
    grad_c_edge = (
        lax.dot_general(
            weighted_grads, state_used, contract_last, preferred_element_type=jnp.float32
        )
        / state_size
    )
    grad_b_edge = lax.dot_general(
        weighted_values, grad_used, contract_last, preferred_element_type=jnp.float32
    )
    edge_values = jnp.dot(b_rows, grad_used, preferred_element_type=jnp.float32).reshape(
        token_count, head_count, -1
    )
    grad_value_edge = (out_weight.T[:, :, None] * edge_values).reshape(token_count, inner_width)
    grad_values = (grad_value_local + grad_value_edge).astype(jnp.bfloat16)
    grad_bc = jnp.concatenate(
        [grad_b_local + grad_b_edge, grad_c_local + grad_c_edge], axis=1
    ).astype(jnp.bfloat16)
    return (grad_values, grad_bc)


def local(hidden_in, values, log_decay, doc_lengths, proj_bc, grad_out):
    token_count = hidden_in.shape[1]
    state_size = proj_bc.shape[1] // 2
    hidden_rows = hidden_in[0]
    first_proj = lax.all_gather(proj_bc, "fsdp", axis=0, tiled=True)
    projected = jnp.dot(hidden_rows, first_proj, preferred_element_type=jnp.float32).astype(
        jnp.bfloat16
    )
    b_rows = projected[:, :state_size]
    c_rows = projected[:, state_size:]
    lengths = doc_lengths[0]
    doc_starts = jnp.cumsum(lengths) - lengths
    first_token = lax.axis_index("ctx") * token_count
    token_places = first_token + jnp.arange(token_count, dtype=jnp.int32)
    doc_ids = jnp.sum((doc_starts[None, :] <= token_places[:, None]).astype(jnp.int32), axis=1)
    prev_doc = jnp.sum((doc_starts <= first_token - 1).astype(jnp.int32))
    terms = block_terms(b_rows, c_rows, values[0], grad_out[0], log_decay[0], doc_ids, prev_doc)
    total_decay = terms[0]
    unit_pair = (jnp.ones_like(total_decay), jnp.zeros_like(terms[1]))
    state_in = entering((total_decay, terms[1]), "ctx", combine_pairs, unit_pair, False)[1]
    grad_after = entering((total_decay, terms[2]), "ctx", combine_pairs, unit_pair, True)[1]
    grad_values, grad_bc = block_finish(b_rows, terms, state_in, grad_after)
    contract_last = (((1,), (1,)), ((), ()))
    grad_hidden = lax.dot_general(
        grad_bc, first_proj, contract_last, preferred_element_type=jnp.float32
    ).astype(jnp.bfloat16)
    seq_total = lax.axis_size("fsdp") * hidden_in.shape[0]
    contract_first = (((0,), (0,)), ((), ()))
    full_term = (
        lax.dot_general(hidden_rows, grad_bc, contract_first, preferred_element_type=jnp.float32)
        / seq_total
    )
    summed = lax.psum(full_term, "ctx")
    grad_proj = lax.psum_scatter(summed, "fsdp", scatter_dimension=0, tiled=True)
    return (grad_values[None], grad_hidden[None], grad_proj)


def solution(mesh):
    in_specs = (
        P("fsdp", "ctx", None),
        P("fsdp", "ctx", None),
        P("fsdp", None, "ctx"),
        P("fsdp", None),
        P("fsdp", None),
        P("fsdp", "ctx", None),
    )
    out_specs = (P("fsdp", "ctx", None), P("fsdp", "ctx", None), P("fsdp", None))
    return jax.shard_map(local, mesh=mesh, in_specs=in_specs, out_specs=out_specs, check_vma=False)
```

profile of v0, /device:TPU:0, one launch (start us, length us, event | category | flops | bytes accessed | tf_op | source)
XLA Modules:
  0.0 186.9 jit_solution(2364739231670539729)
XLA Ops:
  7.2 0.0 all-gather.6.cloned.1.call-start
  7.3 0.8 reduce-window.4
  8.1 0.7 fusion.34
  8.7 0.1 convert_reduce_fusion
  8.8 0.6 slice.16
  9.4 1.3 fusion.33
  10.7 1.0 reduce_window_sum.18
  11.7 0.2 slice_reduce_fusion
  11.9 1.4 copy.36
  13.4 25.1 %all_gather.21 = bf16[1280,256]{1,0:T(8,128)(2,1)S(1)} all-gather(bf16[80,256]{1,0:T(8,128)(2,1)S(1)} %copy-done.8), channel_id=1, replica_groups=mesh['ctx'=2,'fsdp'=16] {'fsdp'}, dimensions={0}, use_global_device_ids=true | all-gather | bytes 696320 | tf_op jit(solution)/shard_map/all_gather | solution.py:148
  38.5 1.3 compare_convert_fusion
  39.8 0.1 multiply_bitcast_fusion
  39.9 0.1 fusion.10
  40.0 0.3 convolution_convert_fusion.2
  40.3 0.5 copy-done.1
  40.9 1.2 fusion.4
  42.1 0.0 all-gather.8.cloned.1.call-start
  42.2 0.3 copy.40
  42.5 0.1 fusion.9
  42.7 0.9 copy-done.2
  43.6 1.2 convolution_convert_fusion
  44.8 0.0 all-gather.8.cloned.1.call-update
  44.8 0.0 reduce-scatter.4.cloned.1.call-start
  46.2 0.1 fusion.24
  46.3 0.2 fusion.32
  46.5 0.6 dynamic-slice
  47.8 0.2 dynamic-update-slice
  48.0 5.1 %all-reduce = bf16[80]{0:T(256)(128)(2,1)S(1)} all-reduce(bf16[80]{0:T(256)(128)(2,1)S(1)} %dynamic-update-slice), channel_id=2, replica_groups=mesh['ctx'=2,'fsdp'=16] {'ctx'}, use_global_device_ids=true, to_apply=%add | all-reduce | flops 80 | bytes 320
  53.1 0.1 reshape.165
  53.2 2.4 %multiply_reduce_fusion = f32[128,128]{1,0:T(8,128)S(1)} fusion(bf16[128,40,64]{0,2,1:T(8,128)(2,1)} %bitcast.81, bf16[128,40,64]{0,2,1:T(8,128)(2,1)} %bitcast.83, f32[40,128]{1,0:T(8,128)S(1)} %reduce_window_sum.18, pred[128,128]{1,0:T(8,128)(4,1)S(1)} %fusion.24), kind=kOutput, calls=%fused_computation.15 | convolution fusion | flops 87146496 | bytes 1413120 | tf_op jit(solution)/shard_map/rhp,thp->hrt/dot_general | solution.py:69
  55.7 8.2 %all-gather.6.cloned.1.call-done = bf16[256,2560]{1,0:T(8,128)(2,1)} async-done(((bf16[128,2560]{1,0:T(8,128)(2,1)}), bf16[256,2560]{1,0:T(8,128)(2,1)}) %all-gather.6.cloned.1.call-update) | async-done | bytes 1310736 | tf_op jit(solution)/shard_map/all_gather | solution.py:10
  63.8 4.2 %while.30 = (s32[]{:T(128)}, f32[128,2560]{1,0:T(8,128)S(1)}, s32[]{:T(128)}, bf16[2,40]{1,0:T(2,128)(2,1)S(1)}, bf16[2,128,2560]{2,1,0:T(8,128)(2,1)}, /*index=5*/s32[]{:T(128)}, s32[]{:T(128)}, s32[]{:T(128)}) while((s32[]{:T(128)}, f32[128,2560]{1,0:T(8,128)S(1)}, s32[]{:T(128)}, bf16[2,40]{1,0:T(2,128)(2,1)S(1)}, ...), condition=%wide.region_5.6_spmd.clone, body=%wide.region_4.5_spmd.clone.sunk | while | flops 1638448 | bytes 3318319 | solution.py:28
  63.9 0.1 mul.206
  63.9 0.1 mul.207
  64.0 1.9 %fusion.51 = f32[128,2560]{1,0:T(8,128)S(1)} fusion(f32[128,2560]{1,0:T(8,128)S(1)} %get-tuple-element.374, bf16[2,128,2560]{2,1,0:T(8,128)(2,1)} %get-tuple-element.385, s32[]{:T(128)S(6)} %select_n.90, f32[2560]{0:T(1024)S(1)} %mul.207, pred[]{:T(512)S(6)} %compare.6, pred[]{:T(512)S(6)} %gt.12), kind=kLoop, calls=%fused_computation.1.clone.1 | loop fusion | flops 1638400 | bytes 3287046 | tf_op jit(solution)/shard_map/while/body/eval_jaxpr/jit(_where)/select_n | solution.py:26
  66.0 0.1 mul.206
  66.0 0.1 mul.207
  66.1 1.9 %fusion.51 = f32[128,2560]{1,0:T(8,128)S(1)} fusion(f32[128,2560]{1,0:T(8,128)S(1)} %get-tuple-element.374, bf16[2,128,2560]{2,1,0:T(8,128)(2,1)} %get-tuple-element.385, s32[]{:T(128)S(6)} %select_n.90, f32[2560]{0:T(1024)S(1)} %mul.207, pred[]{:T(512)S(6)} %compare.6, pred[]{:T(512)S(6)} %gt.12), kind=kLoop, calls=%fused_computation.1.clone.1 | loop fusion | flops 1638400 | bytes 3287046 | tf_op jit(solution)/shard_map/while/body/eval_jaxpr/jit(_where)/select_n | solution.py:26
  68.0 1.5 fusion.21
  69.5 20.1 %all-gather.8.cloned.1.call-done = bf16[256,2560]{1,0:T(8,128)(2,1)} async-done(((bf16[128,2560]{1,0:T(8,128)(2,1)}), bf16[256,2560]{1,0:T(8,128)(2,1)}) %all-gather.8.cloned.1.call-update) | async-done | bytes 1310736 | tf_op jit(solution)/shard_map/all_gather | solution.py:10
  89.6 4.2 %while.31 = (s32[]{:T(128)}, f32[128,2560]{1,0:T(8,128)S(1)}, s32[]{:T(128)}, bf16[2,40]{1,0:T(2,128)(2,1)S(1)}, bf16[2,128,2560]{2,1,0:T(8,128)(2,1)}, /*index=5*/s32[]{:T(128)}, s32[]{:T(128)}) while((s32[]{:T(128)}, f32[128,2560]{1,0:T(8,128)S(1)}, s32[]{:T(128)}, bf16[2,40]{1,0:T(2,128)(2,1)S(1)}, ...), condition=%wide.region_8.9_spmd.clone, body=%wide.region_7.8_spmd.clone.sunk | while | flops 1638444 | bytes 3318265 | solution.py:28
  89.6 0.1 mul.210
  89.6 0.1 mul.211
  89.7 1.9 %fusion.52 = f32[128,2560]{1,0:T(8,128)S(1)} fusion(f32[128,2560]{1,0:T(8,128)S(1)} %get-tuple-element.397, bf16[2,128,2560]{2,1,0:T(8,128)(2,1)} %get-tuple-element.407, s32[]{:T(128)} %get-tuple-element.396, f32[2560]{0:T(1024)S(1)} %mul.211, pred[]{:T(512)S(6)} %compare.7, pred[]{:T(512)S(6)} %lt.45), kind=kLoop, calls=%fused_computation.4.clone.1 | loop fusion | flops 1638400 | bytes 3287046 | tf_op jit(solution)/shard_map/while/body/eval_jaxpr/jit(_where)/select_n | solution.py:26
  91.7 0.1 mul.210
  91.7 0.1 mul.211
  91.8 1.9 %fusion.52 = f32[128,2560]{1,0:T(8,128)S(1)} fusion(f32[128,2560]{1,0:T(8,128)S(1)} %get-tuple-element.397, bf16[2,128,2560]{2,1,0:T(8,128)(2,1)} %get-tuple-element.407, s32[]{:T(128)} %get-tuple-element.396, f32[2560]{0:T(1024)S(1)} %mul.211, pred[]{:T(512)S(6)} %compare.7, pred[]{:T(512)S(6)} %lt.45), kind=kLoop, calls=%fused_computation.4.clone.1 | loop fusion | flops 1638400 | bytes 3287046 | tf_op jit(solution)/shard_map/while/body/eval_jaxpr/jit(_where)/select_n | solution.py:26
  93.7 1.5 convolution_multiply_fusion.4
  95.2 0.2 fusion.16
  95.4 0.1 fusion.17
  95.5 0.4 fusion.6
  95.9 1.5 copy.51
  97.4 0.0 all-reduce.3.cloned.1.call-start
  97.4 0.1 mul.141
  97.5 1.5 copy.38
  99.0 0.1 convolution_multiply_fusion.3
  99.1 2.3 %fusion.8 = f32[40,128,64]{1,2,0:T(8,128)S(1)} fusion(bf16[128,40,64]{0,2,1:T(8,128)(2,1)} %bitcast.82, f32[128,128]{1,0:T(8,128)S(1)} %convolution_multiply_fusion.3, f32[40,128]{1,0:T(8,128)S(1)} %reduce_window_sum.18, pred[128,128]{1,0:T(8,128)(4,1)S(1)} %fusion.24), kind=kOutput, calls=%fused_computation.20 | convolution fusion | flops 87162880 | bytes 2068480 | tf_op jit(solution)/shard_map/hrt,rhp->thp/dot_general | solution.py:73
  101.4 1.5 copy.39
  102.9 3.0 %fusion.5 = bf16[1,128,2560]{2,1,0:T(8,128)(2,1)} fusion(f32[128,2560]{1,0:T(8,128)} %copy.39, f32[128,2560]{1,0:T(8,128)} %copy.38, f32[128,2560]{1,0:T(8,128)S(1)} %get-tuple-element.229, bf16[128,256]{1,0:T(8,128)(2,1)S(1)} %convolution_convert_fusion.2), kind=kOutput, calls=%fused_computation.12 | convolution fusion | flops 85196800 | bytes 4620288 | tf_op jit(solution)/shard_map/dot_general | solution.py:133
  105.9 50.3 %reduce-scatter.4.cloned.1.call-done = f32[80,256]{1,0:T(8,128)} async-done(((f32[1280,256]{1,0:T(8,128)}), f32[80,256]{1,0:T(8,128)}) %reduce-scatter.4.cloned.1.call-update) | async-done | bytes 81936
  156.1 1.6 copy.52
  157.8 1.1 fusion.7
  158.9 19.9 %all-reduce.3.cloned.1.call-done = f32[80,256]{0,1:T(8,128)} async-done(((f32[80,256]{0,1:T(8,128)}), f32[80,256]{0,1:T(8,128)}) %all-reduce.3.cloned.1.call-update) | async-done | bytes 81936 | tf_op jit(solution)/shard_map/psum | solution.py:176
  178.8 1.6 copy.46
  (29 shorter events, 0.1 us)
Async XLA Ops:
  7.2 32.9 %copy-start = (bf16[1,128,1280]{2,1,0:T(8,128)(2,1)S(1)}, bf16[1,128,1280]{2,1,0:T(8,128)(2,1)}, u32[]{:S(2)}) copy-start(bf16[1,128,1280]{2,1,0:T(8,128)(2,1)} %param.10) | copy-start | bytes 983044
  7.2 6.2 %copy-start.8 = (bf16[80,256]{1,0:T(8,128)(2,1)S(1)}, bf16[80,256]{1,0:T(8,128)(2,1)}, u32[]{:S(2)}) copy-start(bf16[80,256]{1,0:T(8,128)(2,1)} %param.14) | copy-start | bytes 122884
  7.2 56.7 %all-gather.6.cloned.1.call-start = ((), (), s32[]{:S(2)}) async-start(), calls=%async_computation.1 | async-start | bytes 1966080 | tf_op jit(solution)/shard_map/all_gather | solution.py:10
  13.3 27.0 %copy-start.5 = (bf16[1,128,2560]{1,2,0:T(8,128)(2,1)}, bf16[1,128,2560]{1,2,0:T(8,128)(2,1)S(1)}, u32[]{:S(2)}) copy-start(bf16[1,128,2560]{1,2,0:T(8,128)(2,1)S(1)} %copy.36) | copy-start | bytes 1966084
  38.5 1.5 copy-start.3
  40.0 0.8 copy-start.1
  40.0 2.1 %copy-start.7 = (bf16[1,128,2560]{2,1,0:T(8,128)(2,1)S(1)}, bf16[1,128,2560]{2,1,0:T(8,128)(2,1)}, u32[]{:S(2)}) copy-start(bf16[1,128,2560]{2,1,0:T(8,128)(2,1)} %param.11) | copy-start | bytes 1966084
  42.1 47.4 %all-gather.8.cloned.1.call-start = ((), (), s32[]{:S(2)}) async-start(), calls=%async_computation.2 | async-start | bytes 1966080 | tf_op jit(solution)/shard_map/all_gather | solution.py:10
  42.5 2.3 %copy-start.6 = (bf16[1,128,2560]{1,2,0:T(8,128)(2,1)}, bf16[1,128,2560]{1,2,0:T(8,128)(2,1)S(1)}, u32[]{:S(2)}) copy-start(bf16[1,128,2560]{1,2,0:T(8,128)(2,1)S(1)} %copy.40) | copy-start | bytes 1966084
  42.6 0.9 copy-start.2
  43.6 2.9 %copy-start.9 = (u32[32]{0:T(128)S(1)}, u32[32]{0:T(128)}, u32[]{:S(2)}) copy-start(u32[32]{0:T(128)} %constant.94) | copy-start | bytes 388
  44.8 111.3 %reduce-scatter.4.cloned.1.call-start = ((), (), s32[]{:S(2)}) async-start(), calls=%async_computation.4 | async-start | bytes 1392640
  97.4 81.4 %all-reduce.3.cloned.1.call-start = ((), (), s32[]{:S(2)}) async-start(), calls=%async_computation.3 | async-start | bytes 262144 | tf_op jit(solution)/shard_map/psum | solution.py:176
  102.9 54.9 %copy-start.4 = (bf16[1280,256]{1,0:T(8,128)(2,1)S(1)}, bf16[1280,256]{1,0:T(8,128)(2,1)}, u32[]{:S(2)}) copy-start(bf16[1280,256]{1,0:T(8,128)(2,1)} %copy-done.3) | copy-start | bytes 1966084
Sparse Core Ops, SparseCore 0:
  42.2 21.5 all-gather.5
  65.4 24.1 all-gather.7
  97.5 58.5 reduce-scatter.3
  158.2 20.5 all-reduce.2
where the time goes:
time: 188 us; the launch traced here: 187 us
  waiting for transfers between devices  98.5 us (52%)
  blocking collectives  30.2 us (16%)
  between operations  16 us (9%)
  matrix products  15.2 us (8%)
  local copies, waits for them, and re-layouts  13.4 us (7%)
  other arithmetic  13.4 us (7%)
    unnamed x5, waiting for transfers between devices  50.3 us
    all_gather x2, waiting for transfers between devices, entering(): lax.all_gather(part.astype(kind), axis)  28.3 us
    all_gather x1, blocking collectives, local(): first_proj = lax.all_gather(proj_bc, 'fsdp', axis=0, tiled=True)  25.1 us
    psum x1, waiting for transfers between devices, local(): summed = lax.psum(full_term, 'ctx')  19.9 us
    unnamed x28, local copies, waits for them, and re-layouts  8.88 us
    select_n x4, other arithmetic, turn(): return jax.tree.map(lambda a, b: jnp.where(reached, a, b), new, before)  7.64 us
    unnamed x1, blocking collectives  5.12 us
  transfers between devices with their start and end apart: 4, of which 4 were waited for; matrix products, arithmetic and copies ran while one was open for 11% of the time, Pallas kernels for 0%

commit v1 on v0

--- a/solution.py
+++ b/solution.py
@@ -173,7 +173,8 @@
         lax.dot_general(hidden_rows, grad_bc, contract_first, preferred_element_type=jnp.float32)
         / seq_total
     )
-    summed = lax.psum(full_term, "ctx")
+    built = lax.all_gather(full_term, axis_name="ctx")
+    summed = jnp.sum(built, axis=0)
     grad_proj = lax.psum_scatter(summed, "fsdp", scatter_dimension=0, tiled=True)
     return (grad_values[None], grad_hidden[None], grad_proj)
 

time: 188 us -> 213 us (1.13)
  waiting for transfers between devices: 98.5 us -> 114 us
  other arithmetic: 13.4 us -> 18.3 us
  local copies, waits for them, and re-layouts: 13.4 us -> 16 us
    all_gather x0 -> x1, waiting for transfers between devices: none -> 38.9 us  [local(): built = lax.all_gather(full_term, axis_name='ctx')]
    psum x1 -> x0, waiting for transfers between devices: 19.9 us -> none  [local(): summed = lax.psum(full_term, 'ctx')]
    reduce_sum x0 -> x1, other arithmetic: none -> 4.85 us  [local(): summed = jnp.sum(built, axis=0)]
    all_gather x0 -> x1, local copies, waits for them, and re-layouts: none -> 4.49 us  [local(): built = lax.all_gather(full_term, axis_name='ctx')]
    unnamed x5, waiting for transfers between devices: 50.3 us -> 47 us
    unnamed x28 -> x26, local copies, waits for them, and re-layouts: 8.88 us -> 5.58 us
where the time goes in v1:
time: 213 us; the launch traced here: 212 us
  waiting for transfers between devices  114 us (54%)
  blocking collectives  30.2 us (14%)
  other arithmetic  18.3 us (9%)
  matrix products  17.1 us (8%)
  local copies, waits for them, and re-layouts  16 us (8%)
  between operations  15.9 us (7%)
    unnamed x5, waiting for transfers between devices  47 us
    all_gather x1, waiting for transfers between devices, local(): built = lax.all_gather(full_term, axis_name='ctx')  38.9 us
    all_gather x2, waiting for transfers between devices, entering(): lax.all_gather(part.astype(kind), axis)  28.3 us
    all_gather x1, blocking collectives, local(): first_proj = lax.all_gather(proj_bc, 'fsdp', axis=0, tiled=True)  25.1 us
    select_n x4, other arithmetic, turn(): return jax.tree.map(lambda a, b: jnp.where(reached, a, b), new, before)  7.64 us
    unnamed x26, local copies, waits for them, and re-layouts  5.58 us
    unnamed x1, blocking collectives  5.12 us
    reduce_sum x1, other arithmetic, local(): summed = jnp.sum(built, axis=0)  4.85 us
  transfers between devices with their start and end apart: 4, of which 4 were waited for; matrix products, arithmetic and copies ran while one was open for 11% of the time, Pallas kernels for 0%

profile of v1, /device:TPU:0, one launch (start us, length us, event | category | flops | bytes accessed | tf_op | source)
XLA Modules:
  0.0 212.3 jit_solution(18342330552148218122)
XLA Ops:
  7.2 0.0 all-gather.8.cloned.1.call-start
  7.3 0.8 reduce-window.4
  8.1 0.7 fusion.34
  8.7 0.1 convert_reduce_fusion
  8.8 0.6 slice.16
  9.4 1.3 fusion.33
  10.7 1.0 reduce_window_sum.18
  11.7 0.2 slice_reduce_fusion
  11.9 1.4 copy.45
  13.4 25.1 %all_gather.27 = bf16[1280,256]{1,0:T(8,128)(2,1)S(1)} all-gather(bf16[80,256]{1,0:T(8,128)(2,1)S(1)} %copy-done.8), channel_id=1, replica_groups=mesh['ctx'=2,'fsdp'=16] {'fsdp'}, dimensions={0}, use_global_device_ids=true | all-gather | bytes 696320 | tf_op jit(solution)/shard_map/all_gather | solution.py:148
  38.5 1.3 compare_convert_fusion
  39.8 0.1 multiply_bitcast_fusion
  39.9 0.1 fusion.10
  40.0 0.3 convolution_convert_fusion.2
  40.3 0.5 copy-done.1
  40.9 1.2 fusion.4
  42.1 0.0 all-gather.10.cloned.1.call-start
  42.2 0.3 copy.49
  42.5 0.1 fusion.9
  42.7 0.9 copy-done.2
  43.6 1.2 convolution_convert_fusion
  44.8 0.0 all-gather.10.cloned.1.call-update
  44.8 0.0 all-gather.12.cloned.1.call-start
  46.1 0.1 fusion.24
  46.2 0.2 fusion.32
  46.4 0.6 dynamic-slice
  47.7 0.2 dynamic-update-slice
  48.0 5.1 %all-reduce = bf16[80]{0:T(256)(128)(2,1)S(1)} all-reduce(bf16[80]{0:T(256)(128)(2,1)S(1)} %dynamic-update-slice), channel_id=2, replica_groups=mesh['ctx'=2,'fsdp'=16] {'ctx'}, use_global_device_ids=true, to_apply=%add | all-reduce | flops 80 | bytes 320
  53.1 0.1 reshape.165
  53.2 2.4 %multiply_reduce_fusion = f32[128,128]{1,0:T(8,128)S(1)} fusion(bf16[128,40,64]{0,2,1:T(8,128)(2,1)} %bitcast.83, bf16[128,40,64]{0,2,1:T(8,128)(2,1)} %bitcast.85, f32[40,128]{1,0:T(8,128)S(1)} %reduce_window_sum.18, pred[128,128]{1,0:T(8,128)(4,1)S(1)} %fusion.24), kind=kOutput, calls=%fused_computation.15 | convolution fusion | flops 87146496 | bytes 1413120 | tf_op jit(solution)/shard_map/rhp,thp->hrt/dot_general | solution.py:69
  55.6 8.2 %all-gather.8.cloned.1.call-done = bf16[256,2560]{1,0:T(8,128)(2,1)} async-done(((bf16[128,2560]{1,0:T(8,128)(2,1)}), bf16[256,2560]{1,0:T(8,128)(2,1)}) %all-gather.8.cloned.1.call-update) | async-done | bytes 1310736 | tf_op jit(solution)/shard_map/all_gather | solution.py:10
  63.8 4.2 %while.30 = (s32[]{:T(128)}, f32[128,2560]{1,0:T(8,128)S(1)}, s32[]{:T(128)}, bf16[2,40]{1,0:T(2,128)(2,1)S(1)}, bf16[2,128,2560]{2,1,0:T(8,128)(2,1)}, /*index=5*/s32[]{:T(128)}, s32[]{:T(128)}, s32[]{:T(128)}) while((s32[]{:T(128)}, f32[128,2560]{1,0:T(8,128)S(1)}, s32[]{:T(128)}, bf16[2,40]{1,0:T(2,128)(2,1)S(1)}, ...), condition=%wide.region_5.6_spmd.clone, body=%wide.region_4.5_spmd.clone.sunk | while | flops 1638448 | bytes 3318319 | solution.py:28
  63.8 0.1 mul.206
  63.9 0.1 mul.207
  64.0 1.9 fusion.51
  65.9 0.1 mul.206
  66.0 0.1 mul.207
  66.1 1.9 fusion.51
  68.0 1.5 fusion.21
  69.5 20.1 %all-gather.10.cloned.1.call-done = bf16[256,2560]{1,0:T(8,128)(2,1)} async-done(((bf16[128,2560]{1,0:T(8,128)(2,1)}), bf16[256,2560]{1,0:T(8,128)(2,1)}) %all-gather.10.cloned.1.call-update) | async-done | bytes 1310736 | tf_op jit(solution)/shard_map/all_gather | solution.py:10
  89.6 4.2 %while.31 = (s32[]{:T(128)}, f32[128,2560]{1,0:T(8,128)S(1)}, s32[]{:T(128)}, bf16[2,40]{1,0:T(2,128)(2,1)S(1)}, bf16[2,128,2560]{2,1,0:T(8,128)(2,1)}, /*index=5*/s32[]{:T(128)}, s32[]{:T(128)}) while((s32[]{:T(128)}, f32[128,2560]{1,0:T(8,128)S(1)}, s32[]{:T(128)}, bf16[2,40]{1,0:T(2,128)(2,1)S(1)}, ...), condition=%wide.region_8.9_spmd.clone, body=%wide.region_7.8_spmd.clone.sunk | while | flops 1638444 | bytes 3318265 | solution.py:28
  89.6 0.1 mul.210
  89.6 0.1 mul.211
  89.7 1.9 fusion.52
  91.7 0.1 mul.210
  91.7 0.1 mul.211
  91.8 1.9 fusion.52
  93.7 1.5 convolution_multiply_fusion.4
  95.2 0.2 fusion.16
  95.4 0.1 fusion.17
  95.5 1.5 fusion.6
  97.0 0.2 reduce-scatter.4.cloned.1.call-start
  97.2 38.9 %all-gather.12.cloned.1.call-done = f32[2560,256]{0,1:T(8,128)} async-done(((f32[1280,256]{0,1:T(8,128)}), f32[2560,256]{0,1:T(8,128)}) %all-gather.12.cloned.1.call-update) | async-done | bytes 2621456 | tf_op jit(solution)/shard_map/all_gather | solution.py:176
  136.1 4.5 %reshape.168 = f32[2,1280,256]{1,0,2:T(2,128)} reshape(f32[2560,256]{0,1:T(8,128)} %all-gather.12.cloned.1.call-done) | data formatting | bytes 5242880 | tf_op jit(solution)/shard_map/all_gather | solution.py:176
  140.6 4.9 %reduce_sum.39 = f32[1280,256]{0,1:T(8,128)S(1)} reduce(f32[2,1280,256]{1,0,2:T(2,128)} %reshape.168, f32[]{:T(128)} %constant.83.clone.1), dimensions={0}, to_apply=%region_9.10 | reduce | flops 327680 | bytes 3932164 | tf_op jit(solution)/shard_map/reduce_sum | solution.py:177
  145.5 1.5 copy.60
  147.0 0.1 mul.141
  147.1 1.5 copy.47
  148.6 0.1 convolution_multiply_fusion.3
  148.7 3.2 %fusion.8 = f32[40,128,64]{1,2,0:T(8,128)} fusion(bf16[128,40,64]{0,2,1:T(8,128)(2,1)} %bitcast.84, f32[128,128]{1,0:T(8,128)S(1)} %convolution_multiply_fusion.3, f32[40,128]{1,0:T(8,128)S(1)} %reduce_window_sum.18, pred[128,128]{1,0:T(8,128)(4,1)S(1)} %fusion.24), kind=kOutput, calls=%fused_computation.20 | convolution fusion | flops 87162880 | bytes 2068480 | tf_op jit(solution)/shard_map/hrt,rhp->thp/dot_general | solution.py:73
  151.9 2.9 %copy.48 = f32[128,2560]{1,0:T(8,128)} copy(f32[128,2560]{0,1:T(8,128)} %bitcast.86) | data formatting | bytes 2621440 | tf_op jit(solution)/shard_map/reshape | solution.py:75
  154.7 1.1 fusion.7
  155.8 2.9 %fusion.5 = bf16[1,128,2560]{2,1,0:T(8,128)(2,1)} fusion(f32[128,2560]{1,0:T(8,128)} %copy.48, f32[128,2560]{1,0:T(8,128)} %copy.47, f32[128,2560]{1,0:T(8,128)S(1)} %get-tuple-element.229, bf16[128,256]{1,0:T(8,128)(2,1)S(1)} %convolution_convert_fusion.2), kind=kOutput, calls=%fused_computation.12 | convolution fusion | flops 85196800 | bytes 4620288 | tf_op jit(solution)/shard_map/dot_general | solution.py:133
  158.8 47.0 %reduce-scatter.4.cloned.1.call-done = f32[80,256]{1,0:T(8,128)} async-done(((f32[1280,256]{1,0:T(8,128)}), f32[80,256]{1,0:T(8,128)}) %reduce-scatter.4.cloned.1.call-update) | async-done | bytes 81936
  (29 shorter events, 0.1 us)
Async XLA Ops:
  7.2 32.9 %copy-start = (bf16[1,128,1280]{2,1,0:T(8,128)(2,1)S(1)}, bf16[1,128,1280]{2,1,0:T(8,128)(2,1)}, u32[]{:S(2)}) copy-start(bf16[1,128,1280]{2,1,0:T(8,128)(2,1)} %param.10) | copy-start | bytes 983044
  7.2 6.2 %copy-start.8 = (bf16[80,256]{1,0:T(8,128)(2,1)S(1)}, bf16[80,256]{1,0:T(8,128)(2,1)}, u32[]{:S(2)}) copy-start(bf16[80,256]{1,0:T(8,128)(2,1)} %param.14) | copy-start | bytes 122884
  7.2 56.7 %all-gather.8.cloned.1.call-start = ((), (), s32[]{:S(2)}) async-start(), calls=%async_computation.1 | async-start | bytes 1966080 | tf_op jit(solution)/shard_map/all_gather | solution.py:10
  13.3 27.0 %copy-start.5 = (bf16[1,128,2560]{1,2,0:T(8,128)(2,1)}, bf16[1,128,2560]{1,2,0:T(8,128)(2,1)S(1)}, u32[]{:S(2)}) copy-start(bf16[1,128,2560]{1,2,0:T(8,128)(2,1)S(1)} %copy.45) | copy-start | bytes 1966084
  38.5 1.5 copy-start.3
  40.0 0.8 copy-start.1
  40.0 2.1 %copy-start.7 = (bf16[1,128,2560]{2,1,0:T(8,128)(2,1)S(1)}, bf16[1,128,2560]{2,1,0:T(8,128)(2,1)}, u32[]{:S(2)}) copy-start(bf16[1,128,2560]{2,1,0:T(8,128)(2,1)} %param.11) | copy-start | bytes 1966084
  42.1 47.4 %all-gather.10.cloned.1.call-start = ((), (), s32[]{:S(2)}) async-start(), calls=%async_computation.2 | async-start | bytes 1966080 | tf_op jit(solution)/shard_map/all_gather | solution.py:10
  42.5 2.3 %copy-start.6 = (bf16[1,128,2560]{1,2,0:T(8,128)(2,1)}, bf16[1,128,2560]{1,2,0:T(8,128)(2,1)S(1)}, u32[]{:S(2)}) copy-start(bf16[1,128,2560]{1,2,0:T(8,128)(2,1)S(1)} %copy.49) | copy-start | bytes 1966084
  42.7 0.9 copy-start.2
  43.6 2.9 %copy-start.9 = (u32[32]{0:T(128)S(1)}, u32[32]{0:T(128)}, u32[]{:S(2)}) copy-start(u32[32]{0:T(128)} %constant.94) | copy-start | bytes 388
  44.8 91.4 %all-gather.12.cloned.1.call-start = ((), (), s32[]{:S(2)}) async-start(), calls=%async_computation.3 | async-start | bytes 3932160 | tf_op jit(solution)/shard_map/all_gather | solution.py:176
  97.0 108.7 %reduce-scatter.4.cloned.1.call-start = ((), (), s32[]{:S(2)}) async-start(), calls=%async_computation.4 | async-start | bytes 1392640
  151.9 2.9 %copy-start.4 = (bf16[1280,256]{1,0:T(8,128)(2,1)S(1)}, bf16[1280,256]{1,0:T(8,128)(2,1)}, u32[]{:S(2)}) copy-start(bf16[1280,256]{1,0:T(8,128)(2,1)} %copy-done.3) | copy-start | bytes 1966084
Sparse Core Ops, SparseCore 0:
  42.2 21.5 all-gather.7
  65.4 24.1 all-gather.9
  97.1 38.9 all-gather.11
  147.1 58.5 reduce-scatter.3
